TPU v7x, 32 devices: a whole 2x2x4 slice. The times are simulated.
32 devices in a mesh: prow: 4 (over z), pcol: 8 (over y, x, core).
Axes of the slice: x: 2, y: 2, z: 4, core: 2. Of those that a mesh axis runs over, the one named last changes fastest.
Arguments:
- matrix: float32 [2048, 8192], P('prow', 'pcol'), may hold values from -6 to 6
- pivot_inverse: float32 [2, 512, 512], P(None, 'prow'), may hold values from -0.01171875 to 0.01171875
- row_live: int32 [2, 4], replicated, may hold values 0 or 1
- col_live: int32 [2, 16], replicated, may hold values 0 or 1
Outputs:
- factored: float32 [2048, 8192], P('prow', 'pcol')
All inputs are finite; a program needn't handle non-finite values.
Results may differ from a plain program's by a relative error of at most 0.0001.
Values sent between devices are 32-bit elements; how exact they have to be, the bound alone decides.
A program may use at most 64 MiB of HBM per device.

v0:
```python
import jax
import jax.numpy as jnp
from jax import lax
from jax.sharding import PartitionSpec as P


def spread(value, axis, source):
    kept = jnp.where(lax.axis_index(axis) == source, value, 0).astype(value.dtype)
    return lax.psum(kept, axis)


def apply_pivot(column_part, pivot_rows):
    return jnp.einsum(
        "rbc,cd->rbd",
        column_part,
        lax.all_gather(pivot_rows, "prow", axis=0, tiled=True),
        precision=lax.Precision.HIGHEST,
    )


def per_device(matrix, pivot_inverse, row_live, col_live):
    block_width = pivot_inverse.shape[2]
    row_blocks = matrix.shape[0] // block_width
    col_blocks = matrix.shape[1] // block_width
    pcol_here = lax.axis_index("pcol")
    row_index = jnp.arange(row_blocks, dtype=jnp.int32) * lax.axis_size("prow") + lax.axis_index(
        "prow"
    )
    col_index = jnp.arange(col_blocks, dtype=jnp.int32) * lax.axis_size("pcol") + pcol_here
    blocks = matrix.reshape(row_blocks, block_width, col_blocks, block_width)

    def lower_panel(column_part, panel):
        row_mask = jnp.where(row_index > panel, jnp.take(row_live[panel], row_index), 0).astype(
            jnp.float32
        )[:, None, None]
        received = spread(column_part, "pcol", panel)
        return apply_pivot(received, pivot_inverse[panel]) * row_mask

    def upper_row(current, panel):
        col_mask = jnp.where(col_index > panel, jnp.take(col_live[panel], col_index), 0).astype(
            jnp.float32
        )
        return spread(current[0] * col_mask[None, :, None], "prow", panel)

    def store_lower(column_part, lower_part, panel):
        keep_rows = (row_index > panel)[:, None, None] & (pcol_here == panel)
        return jnp.where(keep_rows, lower_part, column_part)

    def outer_update(current, lower_part, upper_part):
        return current - jnp.einsum(
            "rbc,cjd->rbjd", lower_part, upper_part, precision=lax.Precision.HIGHEST
        )

    lower_part = lower_panel(blocks[:, :, 0, :], 0)
    upper_part = upper_row(blocks, 0)
    blocks = outer_update(blocks, lower_part, upper_part)
    blocks = blocks.at[:, :, 0, :].set(store_lower(blocks[:, :, 0, :], lower_part, 0))
    next_lower = lower_panel(blocks[:, :, 0, :], 1)
    next_upper = upper_row(blocks, 1)
    blocks = outer_update(blocks, next_lower, next_upper)
    blocks = blocks.at[:, :, 0, :].set(store_lower(blocks[:, :, 0, :], next_lower, 1))
    return blocks.reshape(row_blocks * block_width, col_blocks * block_width)


def solution(mesh):
    in_specs = (P("prow", "pcol"), P(None, "prow", None), P(), P())
    out_specs = P("prow", "pcol")
    return jax.shard_map(
        per_device, mesh=mesh, in_specs=in_specs, out_specs=out_specs, check_vma=False
    )
```

profile of v0, /device:TPU:31, one launch (start us, length us, event | category | flops | bytes accessed | tf_op | source)
XLA Modules:
  0.0 325.9 jit_solution(18202838055574722769)
XLA Ops:
  7.4 3.0 reshape.144
  10.4 0.9 broadcast_select_fusion
  11.3 1.1 copy.19
  12.4 0.0 all-gather.5.cloned.1.call-start
  12.5 0.0 copy-done.1
  12.5 0.9 fusion.12
  13.4 0.0 all-gather.5.cloned.1.call-update
  13.4 0.0 all-reduce.7.cloned.1.call-start
  13.5 1.9 copy.9
  15.5 0.6 gather_fusion
  16.1 1.6 multiply_select_fusion
  17.8 0.0 all-reduce.7.cloned.1.call-update
  17.8 0.0 all-gather.7.cloned.1.call-start
  17.9 0.5 all-gather.7.cloned.1.call-update
  18.4 0.0 all-reduce.9.cloned.1.call-start
  18.5 0.6 fusion.14
  19.7 0.6 gather_fusion.1
  20.4 47.5 %all-reduce.5.cloned.1.call-done = f32[512,512]{1,0:T(8,128)} async-done(((f32[512,512]{1,0:T(8,128)}), f32[512,512]{1,0:T(8,128)}) %all-reduce.5.cloned.1.call-update) | async-done | bytes 1048592 | tf_op jit(solution)/shard_map/psum | solution.py:9
  67.9 3.4 %convolution_multiply_fusion.1 = f32[512,512]{0,1:T(8,128)S(1)} fusion(f32[512,512]{1,0:T(8,128)} %all-reduce.5.cloned.1.call-done, f32[1,512,512]{2,1,0:T(8,128)} %all-gather.5.cloned.1.call-done, f32[]{:T(128)} %bitcast.6), kind=kOutput, calls=%fused_computation.9 | convolution fusion | flops 1610874880 | bytes 3145732 | tf_op jit(solution)/shard_map/rbc,cd->rbd/dot_general | solution.py:13
  71.3 84.9 %all-reduce.7.cloned.1.call-done = f32[512,2,512]{0,2,1:T(8,128)} async-done(((f32[512,2,512]{0,2,1:T(8,128)}), f32[512,2,512]{0,2,1:T(8,128)}) %all-reduce.7.cloned.1.call-update) | async-done | bytes 2097168 | tf_op jit(solution)/shard_map/psum | solution.py:9
  156.2 5.7 %subtract_bitcast_fusion = f32[1,512,2,512]{1,3,2,0:T(8,128)S(1)} fusion(f32[512,2,512]{0,2,1:T(8,128)} %bitcast.66, f32[512,2,512]{0,2,1:T(8,128)} %all-reduce.7.cloned.1.call-done, f32[512,512]{0,1:T(8,128)S(1)} %convolution_multiply_fusion.1), kind=kOutput, calls=%fused_computation.5 | convolution fusion | flops 3221749760 | bytes 7340032 | tf_op jit(solution)/shard_map/rbc,cjd->rbjd/dot_general | solution.py:50
  161.9 1.7 broadcast_select_fusion.1
  163.6 0.2 all-reduce.11.cloned.1.call-start
  163.8 1.3 bitcast_dynamic-update-slice_fusion
  165.1 1.7 fusion
  167.4 0.0 all-gather.7.cloned.1.call-done
  167.4 51.5 %all-reduce.9.cloned.1.call-done = f32[512,512]{0,1:T(8,128)} async-done(((f32[512,512]{0,1:T(8,128)}), f32[512,512]{0,1:T(8,128)}) %all-reduce.9.cloned.1.call-update) | async-done | bytes 1048592 | tf_op jit(solution)/shard_map/psum | solution.py:9
  219.0 3.4 %convolution_multiply_fusion = f32[512,512]{0,1:T(8,128)S(1)} fusion(f32[512,512]{0,1:T(8,128)} %all-reduce.9.cloned.1.call-done, f32[1,512,512]{2,1,0:T(8,128)} %all-gather.7.cloned.1.call-done, f32[]{:T(128)} %bitcast.17), kind=kOutput, calls=%fused_computation.8 | convolution fusion | flops 1610874880 | bytes 3145732 | tf_op jit(solution)/shard_map/rbc,cd->rbd/dot_general | solution.py:13
  222.4 84.7 %all-reduce.11.cloned.1.call-done = f32[512,2,512]{0,2,1:T(8,128)} async-done(((f32[512,2,512]{0,2,1:T(8,128)}), f32[512,2,512]{0,2,1:T(8,128)}) %all-reduce.11.cloned.1.call-update) | async-done | bytes 2097168 | tf_op jit(solution)/shard_map/psum | solution.py:9
  307.1 6.4 %bitcast_subtract_fusion = f32[1,512,2,512]{1,3,2,0:T(8,128)} fusion(f32[1,512,2,512]{1,3,2,0:T(8,128)S(1)} %bitcast_dynamic-update-slice_fusion, f32[512,2,512]{0,2,1:T(8,128)} %all-reduce.11.cloned.1.call-done, f32[512,512]{0,1:T(8,128)S(1)} %convolution_multiply_fusion), kind=kOutput, calls=%fused_computation.2 | convolution fusion | flops 3221749760 | bytes 7340032 | tf_op jit(solution)/shard_map/rbc,cjd->rbjd/dot_general | solution.py:50
  313.5 2.4 fusion.3
  315.9 2.9 copy.12
  (18 shorter events, 0.1 us)
Async XLA Ops:
  7.4 60.5 %all-reduce.5.cloned.1.call-start = ((), (), s32[]{:S(2)}) async-start(), calls=%async_computation | async-start | bytes 2097152 | tf_op jit(solution)/shard_map/psum | solution.py:9
  11.3 1.2 copy-start.1
  12.4 55.5 %all-gather.5.cloned.1.call-start = ((), (), s32[]{:S(2)}) async-start(), calls=%async_computation.4 | async-start | bytes 1310720 | tf_op jit(solution)/shard_map/all_gather | solution.py:16
  13.4 2.0 copy-start.2
  13.4 142.7 %all-reduce.7.cloned.1.call-start = ((), (), s32[]{:S(2)}) async-start(), calls=%async_computation.1 | async-start | bytes 4194304 | tf_op jit(solution)/shard_map/psum | solution.py:9
  15.4 2.4 copy-start
  17.8 0.7 copy-start.3
  17.8 149.6 %all-gather.7.cloned.1.call-start = ((), (), s32[]{:S(2)}) async-start(), calls=%async_computation.5 | async-start | bytes 1310720 | tf_op jit(solution)/shard_map/all_gather | solution.py:16
  18.4 200.5 %all-reduce.9.cloned.1.call-start = ((), (), s32[]{:S(2)}) async-start(), calls=%async_computation.2 | async-start | bytes 2097152 | tf_op jit(solution)/shard_map/psum | solution.py:9
  163.6 143.5 %all-reduce.11.cloned.1.call-start = ((), (), s32[]{:S(2)}) async-start(), calls=%async_computation.3 | async-start | bytes 4194304 | tf_op jit(solution)/shard_map/psum | solution.py:9
Sparse Core Ops, SparseCore 0:
  12.6 55.2 all-reduce.4
  70.2 85.8 all-reduce.6
  163.7 55.2 all-reduce.8
  221.2 85.8 all-reduce.10
Sparse Core Ops, SparseCore 1:
  14.5 27.2 all-gather.4
  43.2 27.2 all-gather.6
where the time goes:
time: 330 us; the launch traced here: 326 us
  waiting for transfers between devices  269 us (82%)
  matrix products  18.9 us (6%)
  between operations  15.9 us (5%)
  local copies, waits for them, and re-layouts  12.4 us (4%)
  other arithmetic  8.97 us (3%)
    psum x4, waiting for transfers between devices, spread(): return lax.psum(kept, axis)  269 us
    dot_general x2, matrix products, outer_update(): jnp.einsum('rbc,cjd->rbjd', lower_part, upper_part, precision=lax.Precisi...  12.1 us
    dot_general x2, matrix products, apply_pivot(): jnp.einsum('rbc,cd->rbd', column_part, lax.all_gather(pivot_rows, 'prow',...  6.81 us
  transfers between devices with their start and end apart: 6, of which 4 were waited for; matrix products, arithmetic and copies ran while one was open for 7% of the time, Pallas kernels for 0%

commit v1 on v0

v1 whole, which is shorter than its diff:
```python
import functools

import jax
import jax.numpy as jnp
from jax import lax
from jax.experimental import pallas as pl
from jax.experimental.pallas import tpu as pltpu
from jax.sharding import PartitionSpec as P

MESH = pl.DeviceIdType.MESH
CORES = 2
CHUNK = 256
PIECES = 8
TAIL = 4


def split(x):
    high = x.astype(jnp.bfloat16)
    return high, (x - high.astype(jnp.float32)).astype(jnp.bfloat16)


def product(left_high, left_low, right_high, right_low):
    dot = functools.partial(jnp.dot, preferred_element_type=jnp.float32)
    return dot(left_high, right_high) + (dot(left_high, right_low) + dot(left_low, right_high))


def kernel(
    n_row, n_col, row_live, col_live, mat, piv, out,
    acc, u, p, a, low, low_high, low_rest, u_high, u_rest,
    acc_sem, out_sem, u_send, u_recv, p_send, p_recv, p_pass, p_passed, p_own,
    a_own, a_send, a_recv, t_send, t_recv, l_send, l_recv, l_pass, l_passed,
):
    z, pcol = lax.axis_index("prow"), lax.axis_index("pcol")
    core, chip = lax.rem(pcol, CORES), lax.div(pcol, CORES)
    n_chip = n_col // CORES
    partner = (z, pcol + 1 - 2 * core)
    width, half = piv.shape[2], piv.shape[2] // CORES
    rows_own = piv.shape[1]
    rows_half = rows_own // CORES
    chunks, _, chunk = acc.shape
    per_block = width // chunk
    pieces = u_send.shape[1] // chunks
    piece = width // pieces
    steps = chunks * pieces
    last = n_row - 1
    first_chip, active, both = chip == 0, z > 0, z > 1

    def remote(src, dst, send, recv, to):
        return pltpu.make_async_remote_copy(
            src_ref=src, dst_ref=dst, send_sem=send, recv_sem=recv, device_id=to, device_id_type=MESH
        )

    def acc_load(j):
        return pltpu.make_async_copy(mat.at[:, pl.ds(j * chunk, chunk)], acc.at[j], acc_sem.at[j])

    def out_store(j):
        return pltpu.make_async_copy(acc.at[j], out.at[:, pl.ds(j * chunk, chunk)], out_sem.at[j])

    def pivot_own(k):
        return pltpu.make_async_copy(piv.at[k], p.at[k, pl.ds(z * rows_own, rows_own)], p_own.at[k])

    def pivot_rows(k, source):
        return p.at[k, pl.ds(pl.multiple_of(source * rows_own + core * rows_half, 8), rows_half)]

    def pivot_send(k, target):
        return remote(
            piv.at[k, pl.ds(pl.multiple_of(core * rows_half, 8), rows_half)],
            pivot_rows(k, z), p_send.at[k, target], p_recv.at[k, z], (target, pcol),
        )

    def pivot_landed(k, source):
        return remote(pivot_rows(k, source), pivot_rows(k, source), p_send.at[k, source], p_recv.at[k, source], (z, pcol))

    def pivot_pass(k, source):
        return remote(pivot_rows(k, source), pivot_rows(k, source), p_pass.at[k, source], p_passed.at[k, source], partner)

    def piece_of(ref, j, r):
        return ref.at[j, pl.ds(pl.multiple_of(r * piece, 8), piece)]

    def relay_copy(k, s):
        place = piece_of(u.at[k], s // pieces, s % pieces)
        return remote(place, place, u_send.at[k, s], u_recv.at[k, s], (z + 1, pcol))

    def origin_copy(k, s):
        j, r = s // pieces, s % pieces
        return remote(piece_of(acc, j, r), piece_of(u.at[k], j, r), u_send.at[k, s], u_recv.at[k, s], (z + 1, pcol))

    def start_of(k):
        return jnp.where(pcol <= k, per_block * pieces, 0)

    def relay(k, begin, end):
        def body(s, carry):
            copy = relay_copy(k, s)
            copy.wait_recv()

            @pl.when(z < last)
            def _():
                copy.start()

            return carry

        lax.fori_loop(jnp.maximum(begin, start_of(k)), end, body, 0)

    def originate(k, begin, end):
        def body(s, carry):
            origin_copy(k, s).start()
            return carry

        lax.fori_loop(jnp.maximum(begin, start_of(k)), end, body, 0)

    def finish_sends(k, copy):
        def body(s, carry):
            copy(k, s).wait_send()
            return carry

        lax.fori_loop(start_of(k), steps, body, 0)

    def own_rows():
        return pl.ds(pl.multiple_of(core * half, 8), half)

    def lower_send(k, target):
        rows = low.at[k, own_rows()]
        return remote(rows, rows, l_send.at[k, target], l_recv.at[k], (z, target * CORES + core))

    def lower_pass(k):
        rows = low.at[k, own_rows()]
        return remote(rows, rows, l_pass.at[k], l_passed.at[k], partner)

    def row_mask(k):
        return row_live[k, z].astype(jnp.float32)

    def gather_pivot(k):
        for source in range(n_row):
            @pl.when(z != source)
            def _():
                pivot_landed(k, source).wait_recv()
                pivot_pass(k, source).start()
        pivot_own(k).wait()
        for source in range(n_row):
            @pl.when(z != source)
            def _():
                pivot_pass(k, source).wait_recv()

    def apply_pivot(k, left):
        left_high, left_low = split(left)
        for q in range(per_block):
            columns = pl.ds(q * chunk, chunk)
            right = split(p[k, :, columns])
            low[k, own_rows(), columns] = row_mask(k) * product(left_high, left_low, *right)
        for target in range(n_chip - 1, 0, -1):
            lower_send(k, target).start()
        lower_pass(k).start()

    def take_lower(k):
        @pl.when(chip > 0)
        def _():
            lower_send(k, 0).wait_recv()
            lower_pass(k).start()

        lower_pass(k).wait_recv()
        low_high[k], low_rest[k] = split(low[k])

    def update(k, j):
        live = col_live[k, pcol + (j // per_block) * n_col].astype(jnp.float32)

        def run():
            u_high[...], u_rest[...] = split(u[k, j])
            for t in range(CORES):
                rows = pl.ds(t * half, half)
                acc[j, rows] -= live * product(low_high[k, rows], low_rest[k, rows], u_high[...], u_rest[...])

        if j < per_block:
            pl.when(pcol > k)(run)
        else:
            run()

    def store_lower(k):
        @pl.when(pcol == k)
        def _():
            for j in range(per_block):
                acc[j] = low[k, :, pl.ds(j * chunk, chunk)]

    for j in range(chunks):
        acc_load(j).start()

    @pl.when(first_chip & active)
    def _():
        for k in range(2):
            pivot_own(k).start()
        pltpu.make_async_copy(mat.at[own_rows(), pl.ds(0, width)], a.at[core], a_own).start()

    barrier = pltpu.get_barrier_semaphore()
    for other in range(n_row):
        @pl.when(z != other)
        def _():
            pl.semaphore_signal(barrier, inc=1, device_id=(other, pcol), device_id_type=MESH)
    for other in range(n_chip):
        @pl.when(chip != other)
        def _():
            pl.semaphore_signal(barrier, inc=1, device_id=(z, other * CORES + core), device_id_type=MESH)
    pl.semaphore_signal(barrier, inc=1, device_id=partner, device_id_type=MESH)
    pl.semaphore_wait(barrier, n_row + n_chip - 1)

    def swap_columns():
        source = mat.at[pl.ds(pl.multiple_of((1 - core) * half, 8), half), pl.ds(0, width)]
        return remote(source, a.at[core], a_send, a_recv, partner)

    def swapped_columns():
        return remote(a.at[1 - core], a.at[1 - core], a_send, a_recv, partner)

    @pl.when(first_chip)
    def _():
        for k in range(2):
            for target in range(n_row - 1, k, -1):
                @pl.when(z != target)
                def _():
                    pivot_send(k, target).start()

        @pl.when(active)
        def _():
            swap_columns().start()

    for j in range(chunks):
        acc_load(j).wait()

    @pl.when(z == 0)
    def _():
        originate(0, 0, steps)
        for j in range(chunks):
            out_store(j).start()

    @pl.when(active)
    def _():
        @pl.when(first_chip)
        def _():
            gather_pivot(0)
            pltpu.make_async_copy(mat.at[own_rows(), pl.ds(0, width)], a.at[core], a_own).wait()
            swapped_columns().wait_recv()
            apply_pivot(0, a[0])

        relay(0, 0, per_block * pieces)

        @pl.when(first_chip & both)
        def _():
            top = u.at[0, pl.ds(0, per_block)]
            copy = remote(top, top, t_send, t_recv, partner)

            @pl.when(core == 1)
            def _():
                copy.start()

            gather_pivot(1)

            @pl.when(core == 0)
            def _():
                copy.wait_recv()

            live = col_live[0, 1].astype(jnp.float32)
            left = split(low[0, own_rows()])
            for q in range(per_block):
                columns = pl.ds(q * chunk, chunk)
                a[1, :, columns] -= live * product(*left, *split(u[0, q]))
            apply_pivot(1, a[1])

            @pl.when(core == 1)
            def _():
                copy.wait_send()

        relay(0, per_block * pieces, steps - TAIL)
        take_lower(0)
        for j in range(chunks - 1):
            update(0, j)
            relay(0, steps - TAIL + j, steps - TAIL + j + 1)
        relay(0, steps - TAIL + chunks - 1, steps)

        @pl.when(z == 1)
        def _():
            @pl.when(z < last)
            def _():
                originate(1, 0, steps - pieces)

            update(0, chunks - 1)

            @pl.when(z < last)
            def _():
                originate(1, steps - pieces, steps)

            store_lower(0)
            for j in range(chunks):
                out_store(j).start()

        @pl.when(both)
        def _():
            relay(1, 0, pieces)
            update(0, chunks - 1)
            relay(1, pieces, steps - pieces)
            take_lower(1)
            for j in range(chunks - 1):
                update(1, j)
                if j == per_block - 1:
                    store_lower(0)
                    store_lower(1)
                    for done in range(per_block):
                        out_store(done).start()
                elif j >= per_block:
                    out_store(j).start()
                relay(1, steps - pieces + 2 * j, steps - pieces + 2 * j + 2)
            relay(1, steps - pieces + 2 * (chunks - 1), steps)
            update(1, chunks - 1)
            out_store(chunks - 1).start()

    @pl.when(z == 0)
    def _():
        finish_sends(0, origin_copy)

    @pl.when(active & (z < last))
    def _():
        finish_sends(0, relay_copy)

        @pl.when(z == 1)
        def _():
            finish_sends(1, origin_copy)

        @pl.when(both)
        def _():
            finish_sends(1, relay_copy)

    @pl.when(first_chip)
    def _():
        for k in range(2):
            for target in range(n_row - 1, k, -1):
                @pl.when(z != target)
                def _():
                    pivot_send(k, target).wait_send()

    @pl.when(first_chip & (z == 1))
    def _():
        pivot_own(1).wait()

    for k in range(2):
        @pl.when(z > k)
        def _():
            lower_pass(k).wait_send()

            @pl.when(first_chip)
            def _():
                for target in range(n_chip - 1, 0, -1):
                    lower_send(k, target).wait_send()
                for source in range(n_row):
                    @pl.when(z != source)
                    def _():
                        pivot_pass(k, source).wait_send()
                if k == 0:
                    swap_columns().wait_send()

    for j in range(chunks):
        out_store(j).wait()


def per_device(n_row, n_col, matrix, pivot_inverse, row_live, col_live):
    rows, columns = matrix.shape
    panels, rows_own, width = pivot_inverse.shape
    chunk = min(CHUNK, width)
    chunks = columns // chunk
    steps = chunks * PIECES
    f32, bf16, dma = jnp.float32, jnp.bfloat16, pltpu.SemaphoreType.DMA
    return pl.pallas_call(
        functools.partial(kernel, n_row, n_col),
        out_shape=jax.ShapeDtypeStruct((rows, columns), f32),
        in_specs=[pl.BlockSpec(memory_space=pltpu.SMEM)] * 2 + [pl.BlockSpec(memory_space=pl.ANY)] * 2,
        out_specs=pl.BlockSpec(memory_space=pl.ANY),
        scratch_shapes=[
            pltpu.VMEM((chunks, rows, chunk), f32),
            pltpu.VMEM((panels, chunks, width, chunk), f32),
            pltpu.VMEM((panels, width, width), f32),
            pltpu.VMEM((CORES, width // CORES, width), f32),
            pltpu.VMEM((panels, width, width), f32),
            pltpu.VMEM((panels, width, width), bf16),
            pltpu.VMEM((panels, width, width), bf16),
            pltpu.VMEM((width, chunk), bf16),
            pltpu.VMEM((width, chunk), bf16),
            dma((chunks,)), dma((chunks,)),
            dma((panels, steps)), dma((panels, steps)),
            dma((panels, n_row)), dma((panels, n_row)), dma((panels, n_row)), dma((panels, n_row)),
            dma((panels,)), dma, dma, dma, dma, dma,
            dma((panels, n_col // CORES)), dma((panels,)), dma((panels,)), dma((panels,)),
        ],
        compiler_params=pltpu.CompilerParams(
            collective_id=0, has_side_effects=True, vmem_limit_bytes=48 << 20
        ),
    )(row_live, col_live, matrix, pivot_inverse)


def solution(mesh):
    n_row, n_col = mesh.shape["prow"], mesh.shape["pcol"]
    return jax.shard_map(
        functools.partial(per_device, n_row, n_col),
        mesh=mesh,
        in_specs=(P("prow", "pcol"), P(None, "prow", None), P(), P()),
        out_specs=P("prow", "pcol"),
        check_vma=False,
    )
```

time: 330 us -> 112 us (0.34); the launches traced: 326 us -> 111 us
  waiting for transfers between devices: 269 us -> 0 us
  Pallas kernels: 0 us -> 106 us
  matrix products: 18.9 us -> 0 us
  between operations: 15.9 us -> 0.01 us
  other arithmetic: 8.97 us -> 0 us
  local copies, waits for them, and re-layouts: 12.4 us -> 5.31 us
    psum x4 -> x0, waiting for transfers between devices: 269 us -> none  [spread(): return lax.psum(kept, axis)]
    pallas_call x0 -> x1, Pallas kernels: none -> 106 us  [per_device(): pl.pallas_call(functools.partial(kernel, n_row, n_col), out_shape=jax.Sha...]
    dot_general x4 -> x0, matrix products: 18.9 us -> none  [the longest x2 12.1 us: outer_update(): jnp.einsum('rbc,cjd->rbjd', lower_part, upper_part, precision=lax.Precisi...]
    select_n x6 -> x0, other arithmetic: 6.54 us -> none  [the longest x4 5.91 us: spread(): jnp.where(lax.axis_index(axis) == source, value, 0).astype(value.dtype)]
    reshape x2 -> x0, local copies, waits for them, and re-layouts: 5.91 us -> none  [the longest x1 3.03 us: per_device(): blocks = matrix.reshape(row_blocks, block_width, col_blocks, block_width)]
  transfers between devices with their start and end apart: 6 -> 0, of which waited for: 4 -> 0; matrix products, arithmetic and copies ran while one was open for 7% -> 0% of each run, Pallas kernels for 0% -> 0%
where the time goes in v1:
time: 112 us; the launch traced here: 111 us
  Pallas kernels  106 us (95%)
  local copies, waits for them, and re-layouts  5.31 us (5%)
    pallas_call x1, Pallas kernels, per_device(): pl.pallas_call(functools.partial(kernel, n_row, n_col), out_shape=jax.Sha...  106 us
    unnamed x9, local copies, waits for them, and re-layouts  5.31 us

profile of v1, /device:TPU:31, one launch (start us, length us, event | category | flops | bytes accessed | tf_op | source)
XLA Modules:
  0.0 111.4 jit_solution(1180192847673981784)
XLA Ops:
  0.0 0.0 copy-start
  0.0 1.6 %copy-done = f32[512,1024]{1,0:T(8,128)S(1)} copy-done((f32[512,1024]{1,0:T(8,128)S(1)}, f32[512,1024]{1,0:T(8,128)}, u32[]{:S(2)}) %copy-start) | copy-done | bytes 2097176
  1.6 0.0 copy-start.1
  1.6 1.0 copy-done.1
  2.6 0.0 copy-start.2
  2.6 0.7 copy-done.2
  3.3 0.0 copy-start.3
  3.3 0.7 copy-done.3
  4.0 106.1 %shard_map.46 = f32[512,1024]{1,0:T(8,128)S(1)} custom-call(s32[2,4]{1,0:T(2,128)S(1)} %copy-done.2, s32[2,16]{1,0:T(2,128)S(1)} %copy-done.3, f32[512,1024]{1,0:T(8,128)S(1)} %copy-done, f32[2,128,512]{2,1,0:T(8,128)S(1)} %copy-done.1), custom_call_target="tpu_custom_call" | custom-call | tf_op jit(solution)/shard_map/pallas_call | solution.py:367
  110.1 1.3 %copy.6 = f32[512,1024]{1,0:T(8,128)} copy(f32[512,1024]{1,0:T(8,128)S(1)} %shard_map.46) | data formatting | bytes 4194304
Async XLA Ops:
  0.0 1.6 %copy-start = (f32[512,1024]{1,0:T(8,128)S(1)}, f32[512,1024]{1,0:T(8,128)}, u32[]{:S(2)}) copy-start(f32[512,1024]{1,0:T(8,128)} %mat.1) | copy-start | bytes 6291460
  1.6 1.0 copy-start.1
  2.6 0.7 copy-start.2
  3.3 0.7 copy-start.3

commit v2 on v1

--- a/solution.py
+++ b/solution.py
@@ -10,8 +10,9 @@
 MESH = pl.DeviceIdType.MESH
 CORES = 2
 CHUNK = 256
-PIECES = 8
+PIECES = 16
 TAIL = 4
+GRANT = 67_043_328
 
 
 def split(x):
@@ -25,9 +26,9 @@
 
 
 def kernel(
-    n_row, n_col, row_live, col_live, mat, piv, out,
-    acc, u, p, a, low, low_high, low_rest, u_high, u_rest,
-    acc_sem, out_sem, u_send, u_recv, p_send, p_recv, p_pass, p_passed, p_own,
+    n_row, n_col, chunk, row_hbm, col_hbm, mat, piv, acc,
+    row_smem, col_smem, u, p, a, low, low_high, low_rest, u_high, u_rest,
+    acc_sem, mask_sem, u_send, u_recv, p_send, p_recv, p_pass, p_passed, p_own,
     a_own, a_send, a_recv, t_send, t_recv, l_send, l_recv, l_pass, l_passed,
 ):
     z, pcol = lax.axis_index("prow"), lax.axis_index("pcol")
@@ -37,7 +38,7 @@
     width, half = piv.shape[2], piv.shape[2] // CORES
     rows_own = piv.shape[1]
     rows_half = rows_own // CORES
-    chunks, _, chunk = acc.shape
+    chunks = acc.shape[1] // chunk
     per_block = width // chunk
     pieces = u_send.shape[1] // chunks
     piece = width // pieces
@@ -50,11 +51,15 @@
             src_ref=src, dst_ref=dst, send_sem=send, recv_sem=recv, device_id=to, device_id_type=MESH
         )
 
-    def acc_load(j):
-        return pltpu.make_async_copy(mat.at[:, pl.ds(j * chunk, chunk)], acc.at[j], acc_sem.at[j])
-
-    def out_store(j):
-        return pltpu.make_async_copy(acc.at[j], out.at[:, pl.ds(j * chunk, chunk)], out_sem.at[j])
+    load = pltpu.make_async_copy(mat, acc, acc_sem)
+    masks = [
+        pltpu.make_async_copy(row_hbm, row_smem, mask_sem.at[0]),
+        pltpu.make_async_copy(col_hbm, col_smem, mask_sem.at[1]),
+    ]
+
+    def columns_of(j):
+        start = j * chunk
+        return pl.ds(start if isinstance(j, int) else pl.multiple_of(start, 128), chunk)
 
     def pivot_own(k):
         return pltpu.make_async_copy(piv.at[k], p.at[k, pl.ds(z * rows_own, rows_own)], p_own.at[k])
@@ -83,7 +88,8 @@
 
     def origin_copy(k, s):
         j, r = s // pieces, s % pieces
-        return remote(piece_of(acc, j, r), piece_of(u.at[k], j, r), u_send.at[k, s], u_recv.at[k, s], (z + 1, pcol))
+        rows = pl.ds(pl.multiple_of(r * piece, 8), piece)
+        return remote(acc.at[rows, columns_of(j)], piece_of(u.at[k], j, r), u_send.at[k, s], u_recv.at[k, s], (z + 1, pcol))
 
     def start_of(k):
         return jnp.where(pcol <= k, per_block * pieces, 0)
@@ -127,7 +133,7 @@
         return remote(rows, rows, l_pass.at[k], l_passed.at[k], partner)
 
     def row_mask(k):
-        return row_live[k, z].astype(jnp.float32)
+        return row_smem[k, z].astype(jnp.float32)
 
     def gather_pivot(k):
         for source in range(n_row):
@@ -161,13 +167,13 @@
         low_high[k], low_rest[k] = split(low[k])
 
     def update(k, j):
-        live = col_live[k, pcol + (j // per_block) * n_col].astype(jnp.float32)
+        live = col_smem[k, pcol + (j // per_block) * n_col].astype(jnp.float32)
 
         def run():
             u_high[...], u_rest[...] = split(u[k, j])
             for t in range(CORES):
                 rows = pl.ds(t * half, half)
-                acc[j, rows] -= live * product(low_high[k, rows], low_rest[k, rows], u_high[...], u_rest[...])
+                acc[rows, columns_of(j)] -= live * product(low_high[k, rows], low_rest[k, rows], u_high[...], u_rest[...])
 
         if j < per_block:
             pl.when(pcol > k)(run)
@@ -177,11 +183,11 @@
     def store_lower(k):
         @pl.when(pcol == k)
         def _():
-            for j in range(per_block):
-                acc[j] = low[k, :, pl.ds(j * chunk, chunk)]
-
-    for j in range(chunks):
-        acc_load(j).start()
+            acc[:, pl.ds(0, width)] = low[k]
+
+    load.start()
+    for copy in masks:
+        copy.start()
 
     @pl.when(first_chip & active)
     def _():
@@ -220,14 +226,13 @@
         def _():
             swap_columns().start()
 
-    for j in range(chunks):
-        acc_load(j).wait()
+    for copy in masks:
+        copy.wait()
+    load.wait()
 
     @pl.when(z == 0)
     def _():
         originate(0, 0, steps)
-        for j in range(chunks):
-            out_store(j).start()
 
     @pl.when(active)
     def _():
@@ -255,7 +260,7 @@
             def _():
                 copy.wait_recv()
 
-            live = col_live[0, 1].astype(jnp.float32)
+            live = col_smem[0, 1].astype(jnp.float32)
             left = split(low[0, own_rows()])
             for q in range(per_block):
                 columns = pl.ds(q * chunk, chunk)
@@ -286,8 +291,6 @@
                 originate(1, steps - pieces, steps)
 
             store_lower(0)
-            for j in range(chunks):
-                out_store(j).start()
 
         @pl.when(both)
         def _():
@@ -300,14 +303,9 @@
                 if j == per_block - 1:
                     store_lower(0)
                     store_lower(1)
-                    for done in range(per_block):
-                        out_store(done).start()
-                elif j >= per_block:
-                    out_store(j).start()
-                relay(1, steps - pieces + 2 * j, steps - pieces + 2 * j + 2)
-            relay(1, steps - pieces + 2 * (chunks - 1), steps)
+                relay(1, steps - pieces + 4 * j, steps - pieces + 4 * j + 4)
+            relay(1, steps - pieces + 4 * (chunks - 1), steps)
             update(1, chunks - 1)
-            out_store(chunks - 1).start()
 
     @pl.when(z == 0)
     def _():
@@ -353,9 +351,6 @@
                 if k == 0:
                     swap_columns().wait_send()
 
-    for j in range(chunks):
-        out_store(j).wait()
-
 
 def per_device(n_row, n_col, matrix, pivot_inverse, row_live, col_live):
     rows, columns = matrix.shape
@@ -365,12 +360,13 @@
     steps = chunks * PIECES
     f32, bf16, dma = jnp.float32, jnp.bfloat16, pltpu.SemaphoreType.DMA
     return pl.pallas_call(
-        functools.partial(kernel, n_row, n_col),
-        out_shape=jax.ShapeDtypeStruct((rows, columns), f32),
-        in_specs=[pl.BlockSpec(memory_space=pltpu.SMEM)] * 2 + [pl.BlockSpec(memory_space=pl.ANY)] * 2,
-        out_specs=pl.BlockSpec(memory_space=pl.ANY),
+        functools.partial(kernel, n_row, n_col, chunk),
+        out_shape=pltpu.VMEM((rows, columns), f32),
+        in_specs=[pl.BlockSpec(memory_space=pltpu.HBM)] * 4,
+        out_specs=pl.BlockSpec(memory_space=pltpu.VMEM),
         scratch_shapes=[
-            pltpu.VMEM((chunks, rows, chunk), f32),
+            pltpu.SMEM(row_live.shape, jnp.int32),
+            pltpu.SMEM(col_live.shape, jnp.int32),
             pltpu.VMEM((panels, chunks, width, chunk), f32),
             pltpu.VMEM((panels, width, width), f32),
             pltpu.VMEM((CORES, width // CORES, width), f32),
@@ -379,14 +375,14 @@
             pltpu.VMEM((panels, width, width), bf16),
             pltpu.VMEM((width, chunk), bf16),
             pltpu.VMEM((width, chunk), bf16),
-            dma((chunks,)), dma((chunks,)),
+            dma, dma((2,)),
             dma((panels, steps)), dma((panels, steps)),
             dma((panels, n_row)), dma((panels, n_row)), dma((panels, n_row)), dma((panels, n_row)),
             dma((panels,)), dma, dma, dma, dma, dma,
             dma((panels, n_col // CORES)), dma((panels,)), dma((panels,)), dma((panels,)),
         ],
         compiler_params=pltpu.CompilerParams(
-            collective_id=0, has_side_effects=True, vmem_limit_bytes=48 << 20
+            collective_id=0, has_side_effects=True, vmem_limit_bytes=GRANT - 4 * rows * columns
         ),
     )(row_live, col_live, matrix, pivot_inverse)
 

time: 112 us -> 107 us (0.955)
  local copies, waits for them, and re-layouts: 5.31 us -> 1.32 us
    unnamed x9 -> x1, local copies, waits for them, and re-layouts: 5.31 us -> 1.32 us
where the time goes in v2:
time: 107 us
  Pallas kernels  105 us (98%)
  local copies, waits for them, and re-layouts  1.32 us (1%)
    pallas_call x1, Pallas kernels, per_device(): pl.pallas_call(functools.partial(kernel, n_row, n_col, chunk), out_shape=...  105 us

profile of v2, /device:TPU:31, one launch (start us, length us, event | category | flops | bytes accessed | tf_op | source)
XLA Modules:
  0.0 106.6 jit_solution(6475093756210370126)
XLA Ops:
  0.0 105.3 %shard_map.46 = f32[512,1024]{1,0:T(8,128)S(1)} custom-call(s32[2,4]{1,0:T(2,128)} %row_hbm.1, s32[2,16]{1,0:T(2,128)} %col_hbm.1, f32[512,1024]{1,0:T(8,128)} %mat.1, f32[2,128,512]{2,1,0:T(8,128)} %piv.1), custom_call_target="tpu_custom_call" | custom-call | tf_op jit(solution)/shard_map/pallas_call | solution.py:362
  105.3 1.3 %copy.6 = f32[512,1024]{1,0:T(8,128)} copy(f32[512,1024]{1,0:T(8,128)S(1)} %shard_map.46) | data formatting | bytes 4194304

commit v3 on v2

--- a/solution.py
+++ b/solution.py
@@ -12,6 +12,7 @@
 CHUNK = 256
 PIECES = 16
 TAIL = 4
+GUESTS = 24
 GRANT = 67_043_328
 
 
@@ -27,9 +28,10 @@
 
 def kernel(
     n_row, n_col, chunk, row_hbm, col_hbm, mat, piv, acc,
-    row_smem, col_smem, u, p, a, low, low_high, low_rest, u_high, u_rest,
+    row_smem, col_smem, u, p, a, guest, low, low_high, low_rest, u_high, u_rest,
     acc_sem, mask_sem, u_send, u_recv, p_send, p_recv, p_pass, p_passed, p_own,
     a_own, a_send, a_recv, t_send, t_recv, l_send, l_recv, l_pass, l_passed,
+    p_up, g_in, g_recv, g_down, g_out,
 ):
     z, pcol = lax.axis_index("prow"), lax.axis_index("pcol")
     core, chip = lax.rem(pcol, CORES), lax.div(pcol, CORES)
@@ -44,7 +46,10 @@
     piece = width // pieces
     steps = chunks * pieces
     last = n_row - 1
+    guests = guest.shape[1]
+    guest_start = (chunks - 2) * pieces
     first_chip, active, both = chip == 0, z > 0, z > 1
+    guest_end = guest_start + jnp.where(chip > 0, guests, 0)
 
     def remote(src, dst, send, recv, to):
         return pltpu.make_async_remote_copy(
@@ -67,11 +72,14 @@
     def pivot_rows(k, source):
         return p.at[k, pl.ds(pl.multiple_of(source * rows_own + core * rows_half, 8), rows_half)]
 
-    def pivot_send(k, target):
+    def pivot_send(k, target, send):
         return remote(
             piv.at[k, pl.ds(pl.multiple_of(core * rows_half, 8), rows_half)],
-            pivot_rows(k, z), p_send.at[k, target], p_recv.at[k, z], (target, pcol),
+            pivot_rows(k, z), send, p_recv.at[k, z], (target, pcol),
         )
+
+    def pivot_relay(k, source, target):
+        return remote(pivot_rows(k, source), pivot_rows(k, source), p_send.at[k, source], p_recv.at[k, source], (target, pcol))
 
     def pivot_landed(k, source):
         return remote(pivot_rows(k, source), pivot_rows(k, source), p_send.at[k, source], p_recv.at[k, source], (z, pcol))
@@ -89,7 +97,7 @@
     def origin_copy(k, s):
         j, r = s // pieces, s % pieces
         rows = pl.ds(pl.multiple_of(r * piece, 8), piece)
-        return remote(acc.at[rows, columns_of(j)], piece_of(u.at[k], j, r), u_send.at[k, s], u_recv.at[k, s], (z + 1, pcol))
+        return remote((acc if k else mat).at[rows, columns_of(j)], piece_of(u.at[k], j, r), u_send.at[k, s], u_recv.at[k, s], (z + 1, pcol))
 
     def start_of(k):
         return jnp.where(pcol <= k, per_block * pieces, 0)
@@ -119,7 +127,56 @@
             copy(k, s).wait_send()
             return carry
 
-        lax.fori_loop(start_of(k), steps, body, 0)
+        if k:
+            lax.fori_loop(start_of(k), guest_start, body, 0)
+            lax.fori_loop(guest_end, steps, body, 0)
+        else:
+            lax.fori_loop(start_of(k), steps, body, 0)
+
+    def guest_in(i):
+        rows = pl.ds(i * piece, piece)
+        source = acc.at[rows, columns_of(guest_start // pieces)]
+        return remote(source, guest.at[chip, i], g_in.at[i], g_recv.at[chip, i], (z, core))
+
+    def guest_down(q, i):
+        return remote(guest.at[q, i], guest.at[q, i], g_down.at[q, i], g_recv.at[q, i], (z + 1, pcol))
+
+    def guest_out(q, i):
+        target = piece_of(u.at[1], guest_start // pieces, i)
+        return remote(guest.at[q, i], target, g_out.at[q, i], u_recv.at[1, guest_start + i], (z, q * CORES + core))
+
+    def pass_guests():
+        def body(t, carry):
+            q, i = 1 + t // guests, t % guests
+            guest_down(q, i).wait_recv()
+
+            @pl.when(z < last)
+            def _():
+                guest_down(q, i).start()
+
+            @pl.when(both)
+            def _():
+                guest_out(q, i).start()
+
+            return carry
+
+        lax.fori_loop(0, (n_chip - 1) * guests, body, 0)
+
+    def finish_guests():
+        def body(t, carry):
+            q, i = 1 + t // guests, t % guests
+
+            @pl.when(z < last)
+            def _():
+                guest_down(q, i).wait_send()
+
+            @pl.when(both)
+            def _():
+                guest_out(q, i).wait_send()
+
+            return carry
+
+        lax.fori_loop(0, (n_chip - 1) * guests, body, 0)
 
     def own_rows():
         return pl.ds(pl.multiple_of(core * half, 8), half)
@@ -135,17 +192,48 @@
     def row_mask(k):
         return row_smem[k, z].astype(jnp.float32)
 
+    def for_sources(k, visit):
+        for distance in range(1, n_row):
+            @pl.when(z - distance >= 0)
+            def _():
+                visit(z - distance, z + 1, z < last, z > k)
+
+            @pl.when((z + distance <= last) & (z > k))
+            def _():
+                visit(z + distance, z - 1, z - 1 > k, z > k)
+
+    def relay_pivot(k):
+        def visit(source, target, onward, used):
+            pivot_landed(k, source).wait_recv()
+
+            @pl.when(onward)
+            def _():
+                pivot_relay(k, source, target).start()
+
+            @pl.when(used)
+            def _():
+                pivot_pass(k, source).start()
+
+        for_sources(k, visit)
+
     def gather_pivot(k):
-        for source in range(n_row):
-            @pl.when(z != source)
-            def _():
-                pivot_landed(k, source).wait_recv()
-                pivot_pass(k, source).start()
         pivot_own(k).wait()
         for source in range(n_row):
             @pl.when(z != source)
             def _():
                 pivot_pass(k, source).wait_recv()
+
+    def finish_pivot(k):
+        def visit(source, target, onward, used):
+            @pl.when(onward)
+            def _():
+                pivot_relay(k, source, target).wait_send()
+
+            @pl.when(used)
+            def _():
+                pivot_pass(k, source).wait_send()
+
+        for_sources(k, visit)
 
     def apply_pivot(k, left):
         left_high, left_low = split(left)
@@ -166,14 +254,16 @@
         lower_pass(k).wait_recv()
         low_high[k], low_rest[k] = split(low[k])
 
-    def update(k, j):
+    def update(k, j, part=0, parts=1):
         live = col_smem[k, pcol + (j // per_block) * n_col].astype(jnp.float32)
 
         def run():
-            u_high[...], u_rest[...] = split(u[k, j])
+            depth = pl.ds(part * (width // parts), width // parts)
+            u_high[depth], u_rest[depth] = split(u[k, j, depth])
             for t in range(CORES):
                 rows = pl.ds(t * half, half)
-                acc[rows, columns_of(j)] -= live * product(low_high[k, rows], low_rest[k, rows], u_high[...], u_rest[...])
+                left = low_high[k, rows, depth], low_rest[k, rows, depth]
+                acc[rows, columns_of(j)] -= live * product(*left, u_high[depth], u_rest[depth])
 
         if j < per_block:
             pl.when(pcol > k)(run)
@@ -217,31 +307,36 @@
     @pl.when(first_chip)
     def _():
         for k in range(2):
-            for target in range(n_row - 1, k, -1):
-                @pl.when(z != target)
-                def _():
-                    pivot_send(k, target).start()
+            @pl.when(z < last)
+            def _():
+                pivot_send(k, z + 1, p_send.at[k, z]).start()
+
+            @pl.when(z - 1 > k)
+            def _():
+                pivot_send(k, z - 1, p_up.at[k]).start()
 
         @pl.when(active)
         def _():
             swap_columns().start()
+
+    @pl.when(z == 0)
+    def _():
+        originate(0, 0, steps)
 
     for copy in masks:
         copy.wait()
     load.wait()
 
-    @pl.when(z == 0)
-    def _():
-        originate(0, 0, steps)
-
     @pl.when(active)
     def _():
         @pl.when(first_chip)
         def _():
+            relay_pivot(0)
             gather_pivot(0)
             pltpu.make_async_copy(mat.at[own_rows(), pl.ds(0, width)], a.at[core], a_own).wait()
             swapped_columns().wait_recv()
             apply_pivot(0, a[0])
+            relay_pivot(1)
 
         relay(0, 0, per_block * pieces)
 
@@ -282,7 +377,17 @@
         def _():
             @pl.when(z < last)
             def _():
-                originate(1, 0, steps - pieces)
+                @pl.when(chip > 0)
+                def _():
+                    for i in range(guests):
+                        guest_in(i).start()
+
+                originate(1, 0, guest_start)
+                originate(1, guest_end, steps - pieces)
+
+                @pl.when(first_chip)
+                def _():
+                    pass_guests()
 
             update(0, chunks - 1)
 
@@ -296,21 +401,46 @@
         def _():
             relay(1, 0, pieces)
             update(0, chunks - 1)
-            relay(1, pieces, steps - pieces)
+            relay(1, pieces, guest_start)
             take_lower(1)
-            for j in range(chunks - 1):
+            update(1, 0)
+            relay(1, guest_end, guest_end + 4)
+            update(1, 1)
+            store_lower(0)
+            store_lower(1)
+            relay(1, guest_end + 4, steps - pieces)
+
+            @pl.when(first_chip)
+            def _():
+                pass_guests()
+
+            @pl.when(chip > 0)
+            def _():
+                for i in range(guests):
+                    relay_copy(1, guest_start + i).wait_recv()
+
+            for j in range(2, chunks - 1):
                 update(1, j)
-                if j == per_block - 1:
-                    store_lower(0)
-                    store_lower(1)
-                relay(1, steps - pieces + 4 * j, steps - pieces + 4 * j + 4)
-            relay(1, steps - pieces + 4 * (chunks - 1), steps)
-            update(1, chunks - 1)
+            for part in range(4):
+                begin = steps - pieces + part * (pieces // 4)
+                relay(1, begin, begin + pieces // 4)
+                update(1, chunks - 1, part, 4)
 
     @pl.when(z == 0)
     def _():
         finish_sends(0, origin_copy)
 
+    @pl.when(active & first_chip)
+    def _():
+        @pl.when((z < last) | both)
+        def _():
+            finish_guests()
+
+    @pl.when((z == 1) & (z < last) & (chip > 0))
+    def _():
+        for i in range(guests):
+            guest_in(i).wait_send()
+
     @pl.when(active & (z < last))
     def _():
         finish_sends(0, relay_copy)
@@ -326,10 +456,15 @@
     @pl.when(first_chip)
     def _():
         for k in range(2):
-            for target in range(n_row - 1, k, -1):
-                @pl.when(z != target)
-                def _():
-                    pivot_send(k, target).wait_send()
+            @pl.when(z < last)
+            def _():
+                pivot_send(k, z + 1, p_send.at[k, z]).wait_send()
+
+            @pl.when(z - 1 > k)
+            def _():
+                pivot_send(k, z - 1, p_up.at[k]).wait_send()
+
+            finish_pivot(k)
 
     @pl.when(first_chip & (z == 1))
     def _():
@@ -344,10 +479,6 @@
             def _():
                 for target in range(n_chip - 1, 0, -1):
                     lower_send(k, target).wait_send()
-                for source in range(n_row):
-                    @pl.when(z != source)
-                    def _():
-                        pivot_pass(k, source).wait_send()
                 if k == 0:
                     swap_columns().wait_send()
 
@@ -358,6 +489,8 @@
     chunk = min(CHUNK, width)
     chunks = columns // chunk
     steps = chunks * PIECES
+    n_chip = n_col // CORES
+    guests = max(1, GUESTS // n_chip)
     f32, bf16, dma = jnp.float32, jnp.bfloat16, pltpu.SemaphoreType.DMA
     return pl.pallas_call(
         functools.partial(kernel, n_row, n_col, chunk),
@@ -370,6 +503,7 @@
             pltpu.VMEM((panels, chunks, width, chunk), f32),
             pltpu.VMEM((panels, width, width), f32),
             pltpu.VMEM((CORES, width // CORES, width), f32),
+            pltpu.VMEM((n_chip, guests, width // PIECES, chunk), f32),
             pltpu.VMEM((panels, width, width), f32),
             pltpu.VMEM((panels, width, width), bf16),
             pltpu.VMEM((panels, width, width), bf16),
@@ -380,6 +514,7 @@
             dma((panels, n_row)), dma((panels, n_row)), dma((panels, n_row)), dma((panels, n_row)),
             dma((panels,)), dma, dma, dma, dma, dma,
             dma((panels, n_col // CORES)), dma((panels,)), dma((panels,)), dma((panels,)),
+            dma((panels,)), dma((guests,)), dma((n_chip, guests)), dma((n_chip, guests)), dma((n_chip, guests)),
         ],
         compiler_params=pltpu.CompilerParams(
             collective_id=0, has_side_effects=True, vmem_limit_bytes=GRANT - 4 * rows * columns

time: 107 us -> 109 us (1.019)
  the two profiles are of different devices: /device:TPU:31 before, /device:TPU:24 now
where the time goes in v3:
time: 109 us
  Pallas kernels  107 us (98%)
  local copies, waits for them, and re-layouts  1.32 us (1%)
    pallas_call x1, Pallas kernels, per_device(): pl.pallas_call(functools.partial(kernel, n_row, n_col, chunk), out_shape=...  107 us

profile of v3, /device:TPU:24, one launch (start us, length us, event | category | flops | bytes accessed | tf_op | source)
XLA Modules:
  0.0 108.6 jit_solution(12250854338236775399)
XLA Ops:
  0.0 107.2 %shard_map.46 = f32[512,1024]{1,0:T(8,128)S(1)} custom-call(s32[2,4]{1,0:T(2,128)} %row_hbm.1, s32[2,16]{1,0:T(2,128)} %col_hbm.1, f32[512,1024]{1,0:T(8,128)} %mat.1, f32[2,128,512]{2,1,0:T(8,128)} %piv.1), custom_call_target="tpu_custom_call" | custom-call | tf_op jit(solution)/shard_map/pallas_call | solution.py:495
  107.2 1.3 %copy.6 = f32[512,1024]{1,0:T(8,128)} copy(f32[512,1024]{1,0:T(8,128)S(1)} %shard_map.46) | data formatting | bytes 4194304

commit v4 on v3

--- a/solution.py
+++ b/solution.py
@@ -97,7 +97,7 @@
     def origin_copy(k, s):
         j, r = s // pieces, s % pieces
         rows = pl.ds(pl.multiple_of(r * piece, 8), piece)
-        return remote((acc if k else mat).at[rows, columns_of(j)], piece_of(u.at[k], j, r), u_send.at[k, s], u_recv.at[k, s], (z + 1, pcol))
+        return remote(acc.at[rows, columns_of(j)], piece_of(u.at[k], j, r), u_send.at[k, s], u_recv.at[k, s], (z + 1, pcol))
 
     def start_of(k):
         return jnp.where(pcol <= k, per_block * pieces, 0)
@@ -319,13 +319,14 @@
         def _():
             swap_columns().start()
 
+    load.wait()
+
     @pl.when(z == 0)
     def _():
         originate(0, 0, steps)
 
     for copy in masks:
         copy.wait()
-    load.wait()
 
     @pl.when(active)
     def _():
@@ -338,7 +339,8 @@
             apply_pivot(0, a[0])
             relay_pivot(1)
 
-        relay(0, 0, per_block * pieces)
+        ahead = jnp.where(pcol == 0, steps - TAIL, per_block * pieces)
+        relay(0, 0, ahead)
 
         @pl.when(first_chip & both)
         def _():
@@ -366,7 +368,7 @@
             def _():
                 copy.wait_send()
 
-        relay(0, per_block * pieces, steps - TAIL)
+        relay(0, ahead, steps - TAIL)
         take_lower(0)
         for j in range(chunks - 1):
             update(0, j)

time: 109 us -> 104 us (0.954)
  the two profiles are of different devices: /device:TPU:24 before, /device:TPU:31 now
where the time goes in v4:
time: 104 us; the launch traced here: 103 us
  Pallas kernels  102 us (98%)
  local copies, waits for them, and re-layouts  1.32 us (1%)
    pallas_call x1, Pallas kernels, per_device(): pl.pallas_call(functools.partial(kernel, n_row, n_col, chunk), out_shape=...  102 us

profile of v4, /device:TPU:31, one launch (start us, length us, event | category | flops | bytes accessed | tf_op | source)
XLA Modules:
  0.0 102.8 jit_solution(16636144463471642040)
XLA Ops:
  0.0 101.5 %shard_map.46 = f32[512,1024]{1,0:T(8,128)S(1)} custom-call(s32[2,4]{1,0:T(2,128)} %row_hbm.1, s32[2,16]{1,0:T(2,128)} %col_hbm.1, f32[512,1024]{1,0:T(8,128)} %mat.1, f32[2,128,512]{2,1,0:T(8,128)} %piv.1), custom_call_target="tpu_custom_call" | custom-call | tf_op jit(solution)/shard_map/pallas_call | solution.py:497
  101.5 1.3 %copy.6 = f32[512,1024]{1,0:T(8,128)} copy(f32[512,1024]{1,0:T(8,128)S(1)} %shard_map.46) | data formatting | bytes 4194304

commit v5 on v4

--- a/solution.py
+++ b/solution.py
@@ -12,7 +12,7 @@
 CHUNK = 256
 PIECES = 16
 TAIL = 4
-GUESTS = 24
+GUESTS = 32
 GRANT = 67_043_328
 
 
@@ -56,7 +56,6 @@
             src_ref=src, dst_ref=dst, send_sem=send, recv_sem=recv, device_id=to, device_id_type=MESH
         )
 
-    load = pltpu.make_async_copy(mat, acc, acc_sem)
     masks = [
         pltpu.make_async_copy(row_hbm, row_smem, mask_sem.at[0]),
         pltpu.make_async_copy(col_hbm, col_smem, mask_sem.at[1]),
@@ -65,6 +64,9 @@
     def columns_of(j):
         start = j * chunk
         return pl.ds(start if isinstance(j, int) else pl.multiple_of(start, 128), chunk)
+
+    def load(j):
+        return pltpu.make_async_copy(mat.at[:, columns_of(j)], acc.at[:, columns_of(j)], acc_sem.at[j])
 
     def pivot_own(k):
         return pltpu.make_async_copy(piv.at[k], p.at[k, pl.ds(z * rows_own, rows_own)], p_own.at[k])
@@ -275,7 +277,23 @@
         def _():
             acc[:, pl.ds(0, width)] = low[k]
 
-    load.start()
+    barrier = pltpu.get_barrier_semaphore()
+    relays_guests = (z == 1) & (z < last)
+
+    def greet(condition, device):
+        @pl.when(condition)
+        def _():
+            pl.semaphore_signal(barrier, inc=1, device_id=device, device_id_type=MESH)
+
+    greet(active, (z - 1, pcol))
+    greet(active, partner)
+    greet(active & (z < last) & first_chip, (z + 1, pcol))
+    greet(active & (chip > 0), (z, core))
+    for other in range(1, n_chip):
+        greet(relays_guests & first_chip, (z, other * CORES + core))
+
+    for j in range(chunks):
+        load(j).start()
     for copy in masks:
         copy.start()
 
@@ -285,17 +303,14 @@
             pivot_own(k).start()
         pltpu.make_async_copy(mat.at[own_rows(), pl.ds(0, width)], a.at[core], a_own).start()
 
-    barrier = pltpu.get_barrier_semaphore()
-    for other in range(n_row):
-        @pl.when(z != other)
-        def _():
-            pl.semaphore_signal(barrier, inc=1, device_id=(other, pcol), device_id_type=MESH)
-    for other in range(n_chip):
-        @pl.when(chip != other)
-        def _():
-            pl.semaphore_signal(barrier, inc=1, device_id=(z, other * CORES + core), device_id_type=MESH)
-    pl.semaphore_signal(barrier, inc=1, device_id=partner, device_id_type=MESH)
-    pl.semaphore_wait(barrier, n_row + n_chip - 1)
+    targets = (
+        jnp.where(z < last, 1, 0)
+        + jnp.where(active, 1, 0)
+        + jnp.where(both & first_chip, 1, 0)
+        + jnp.where(active & first_chip, n_chip - 1, 0)
+        + jnp.where(relays_guests & (chip > 0), 1, 0)
+    )
+    pl.semaphore_wait(barrier, targets)
 
     def swap_columns():
         source = mat.at[pl.ds(pl.multiple_of((1 - core) * half, 8), half), pl.ds(0, width)]
@@ -319,11 +334,12 @@
         def _():
             swap_columns().start()
 
-    load.wait()
-
-    @pl.when(z == 0)
-    def _():
-        originate(0, 0, steps)
+    for j in range(chunks):
+        load(j).wait()
+
+        @pl.when(z == 0)
+        def _():
+            originate(0, j * pieces, (j + 1) * pieces)
 
     for copy in masks:
         copy.wait()
@@ -511,7 +527,7 @@
             pltpu.VMEM((panels, width, width), bf16),
             pltpu.VMEM((width, chunk), bf16),
             pltpu.VMEM((width, chunk), bf16),
-            dma, dma((2,)),
+            dma((chunks,)), dma((2,)),
             dma((panels, steps)), dma((panels, steps)),
             dma((panels, n_row)), dma((panels, n_row)), dma((panels, n_row)), dma((panels, n_row)),
             dma((panels,)), dma, dma, dma, dma, dma,

time: 104 us -> 103 us (level)
  no operation moved by 1% of the time
where the time goes in v5:
time: 103 us; the launch traced here: 102 us
  Pallas kernels  101 us (98%)
  local copies, waits for them, and re-layouts  1.32 us (1%)
    pallas_call x1, Pallas kernels, per_device(): pl.pallas_call(functools.partial(kernel, n_row, n_col, chunk), out_shape=...  101 us

profile of v5, /device:TPU:31, one launch (start us, length us, event | category | flops | bytes accessed | tf_op | source)
XLA Modules:
  0.0 102.0 jit_solution(4813803632518756448)
XLA Ops:
  0.0 100.7 %shard_map.46 = f32[512,1024]{1,0:T(8,128)S(1)} custom-call(s32[2,4]{1,0:T(2,128)} %row_hbm.1, s32[2,16]{1,0:T(2,128)} %col_hbm.1, f32[512,1024]{1,0:T(8,128)} %mat.1, f32[2,128,512]{2,1,0:T(8,128)} %piv.1), custom_call_target="tpu_custom_call" | custom-call | tf_op jit(solution)/shard_map/pallas_call | solution.py:513
  100.7 1.3 %copy.6 = f32[512,1024]{1,0:T(8,128)} copy(f32[512,1024]{1,0:T(8,128)S(1)} %shard_map.46) | data formatting | bytes 4194304

commit v6 on v5

--- a/solution.py
+++ b/solution.py
@@ -12,7 +12,8 @@
 CHUNK = 256
 PIECES = 16
 TAIL = 4
-GUESTS = 32
+GUESTS = 44
+FEWER = 20
 GRANT = 67_043_328
 
 
@@ -46,7 +47,7 @@
     piece = width // pieces
     steps = chunks * pieces
     last = n_row - 1
-    guests = guest.shape[1]
+    guests = guest.shape[1] - core * (FEWER // n_chip)
     guest_start = (chunks - 2) * pieces
     first_chip, active, both = chip == 0, z > 0, z > 1
     guest_end = guest_start + jnp.where(chip > 0, guests, 0)
@@ -136,7 +137,7 @@
             lax.fori_loop(start_of(k), steps, body, 0)
 
     def guest_in(i):
-        rows = pl.ds(i * piece, piece)
+        rows = pl.ds(pl.multiple_of(i * piece, 8), piece)
         source = acc.at[rows, columns_of(guest_start // pieces)]
         return remote(source, guest.at[chip, i], g_in.at[i], g_recv.at[chip, i], (z, core))
 
@@ -148,37 +149,43 @@
         return remote(guest.at[q, i], target, g_out.at[q, i], u_recv.at[1, guest_start + i], (z, q * CORES + core))
 
     def pass_guests():
-        def body(t, carry):
-            q, i = 1 + t // guests, t % guests
-            guest_down(q, i).wait_recv()
-
-            @pl.when(z < last)
-            def _():
-                guest_down(q, i).start()
-
-            @pl.when(both)
-            def _():
-                guest_out(q, i).start()
+        def body(i, carry):
+            for q in range(1, n_chip):
+                guest_down(q, i).wait_recv()
+
+                @pl.when(z < last)
+                def _():
+                    guest_down(q, i).start()
+
+                @pl.when(both)
+                def _():
+                    guest_out(q, i).start()
 
             return carry
 
-        lax.fori_loop(0, (n_chip - 1) * guests, body, 0)
+        lax.fori_loop(0, guests, body, 0)
 
     def finish_guests():
-        def body(t, carry):
-            q, i = 1 + t // guests, t % guests
-
-            @pl.when(z < last)
-            def _():
-                guest_down(q, i).wait_send()
-
-            @pl.when(both)
-            def _():
-                guest_out(q, i).wait_send()
+        def body(i, carry):
+            for q in range(1, n_chip):
+                @pl.when(z < last)
+                def _():
+                    guest_down(q, i).wait_send()
+
+                @pl.when(both)
+                def _():
+                    guest_out(q, i).wait_send()
 
             return carry
 
-        lax.fori_loop(0, (n_chip - 1) * guests, body, 0)
+        lax.fori_loop(0, guests, body, 0)
+
+    def each_guest(act):
+        def body(i, carry):
+            act(i)
+            return carry
+
+        lax.fori_loop(0, guests, body, 0)
 
     def own_rows():
         return pl.ds(pl.multiple_of(core * half, 8), half)
@@ -397,8 +404,7 @@
             def _():
                 @pl.when(chip > 0)
                 def _():
-                    for i in range(guests):
-                        guest_in(i).start()
+                    each_guest(lambda i: guest_in(i).start())
 
                 originate(1, 0, guest_start)
                 originate(1, guest_end, steps - pieces)
@@ -434,8 +440,7 @@
 
             @pl.when(chip > 0)
             def _():
-                for i in range(guests):
-                    relay_copy(1, guest_start + i).wait_recv()
+                each_guest(lambda i: relay_copy(1, guest_start + i).wait_recv())
 
             for j in range(2, chunks - 1):
                 update(1, j)
@@ -456,8 +461,7 @@
 
     @pl.when((z == 1) & (z < last) & (chip > 0))
     def _():
-        for i in range(guests):
-            guest_in(i).wait_send()
+        each_guest(lambda i: guest_in(i).wait_send())
 
     @pl.when(active & (z < last))
     def _():

time: 103 us -> 105 us (1.019)
  the two profiles are of different devices: /device:TPU:31 before, /device:TPU:25 now
where the time goes in v6:
time: 105 us; the launch traced here: 104 us
  Pallas kernels  103 us (98%)
  local copies, waits for them, and re-layouts  1.32 us (1%)
    pallas_call x1, Pallas kernels, per_device(): pl.pallas_call(functools.partial(kernel, n_row, n_col, chunk), out_shape=...  103 us

profile of v6, /device:TPU:25, one launch (start us, length us, event | category | flops | bytes accessed | tf_op | source)
XLA Modules:
  0.0 104.4 jit_solution(11454808299032384353)
XLA Ops:
  0.0 103.0 %shard_map.46 = f32[512,1024]{1,0:T(8,128)S(1)} custom-call(s32[2,4]{1,0:T(2,128)} %row_hbm.1, s32[2,16]{1,0:T(2,128)} %col_hbm.1, f32[512,1024]{1,0:T(8,128)} %mat.1, f32[2,128,512]{2,1,0:T(8,128)} %piv.1), custom_call_target="tpu_custom_call" | custom-call | tf_op jit(solution)/shard_map/pallas_call | solution.py:517
  103.1 1.3 %copy.6 = f32[512,1024]{1,0:T(8,128)} copy(f32[512,1024]{1,0:T(8,128)S(1)} %shard_map.46) | data formatting | bytes 4194304

commit v7 on v5

--- a/solution.py
+++ b/solution.py
@@ -12,7 +12,7 @@
 CHUNK = 256
 PIECES = 16
 TAIL = 4
-GUESTS = 32
+GUESTS = 28
 GRANT = 67_043_328
 
 

time: 103 us -> 101 us (0.981); the launches traced: 102 us -> 101 us
  Pallas kernels: 101 us -> 99.9 us
where the time goes in v7:
time: 101 us
  Pallas kernels  99.9 us (99%)
  local copies, waits for them, and re-layouts  1.32 us (1%)
    pallas_call x1, Pallas kernels, per_device(): pl.pallas_call(functools.partial(kernel, n_row, n_col, chunk), out_shape=...  99.9 us

profile of v7, /device:TPU:31, one launch (start us, length us, event | category | flops | bytes accessed | tf_op | source)
XLA Modules:
  0.0 101.2 jit_solution(16979169664382673360)
XLA Ops:
  0.0 99.9 %shard_map.46 = f32[512,1024]{1,0:T(8,128)S(1)} custom-call(s32[2,4]{1,0:T(2,128)} %row_hbm.1, s32[2,16]{1,0:T(2,128)} %col_hbm.1, f32[512,1024]{1,0:T(8,128)} %mat.1, f32[2,128,512]{2,1,0:T(8,128)} %piv.1), custom_call_target="tpu_custom_call" | custom-call | tf_op jit(solution)/shard_map/pallas_call | solution.py:513
  99.9 1.3 %copy.6 = f32[512,1024]{1,0:T(8,128)} copy(f32[512,1024]{1,0:T(8,128)S(1)} %shard_map.46) | data formatting | bytes 4194304
